TPU v7x, 32 devices: a whole 2x2x4 slice. The times are simulated.
32 devices in a mesh: sector: 4 (over z), group: 8 (over y, x, core).
Axes of the slice: x: 2, y: 2, z: 4, core: 2. Of those that a mesh axis runs over, the one named last changes fastest.
Arguments:
- spectrum: float32 [1152, 128, 512], P('group', None, 'sector'), may hold values from 0.1 to 2
- land_mask: int32 [128, 512], P(None, 'sector'), may hold values 0 or 1
- wind_field: float32 [2, 128, 512], P(None, 'group', 'sector'), may hold values from -3 to 3
- assignment: int32 [1152], replicated, may hold values from 0 to 1151, each once
- courant: float32 [32], replicated, may hold values from 0.3 to 0.65
- growth: float32 [32], replicated, may hold values from 0.1 to 0.5
- whitecap: float32 [32], replicated, may hold values from 0.2 to 1
- weights: float32 [32], replicated, may hold values from 0.5 to 5
- spread: float32 [32, 36, 36], replicated, may hold values from -1 to 1
Outputs:
- updated: float32 [1152, 128, 512], P('group', None, 'sector')
Inputs may be any that keep to these rules, and one draw needn't show every extreme that they name: `assignment`: each component number appears exactly once.
All inputs are finite; a program needn't handle non-finite values. No bound on the sum of `land_mask` on one device may be relied on, other than what follows from the above.
Results may differ from a plain program's by a relative error of at most 0.00007.
Values sent between devices are 32-bit elements; how exact they have to be, the bound alone decides.
No kernel may reach another device: no remote copies, remote signals or barrier semaphores. Data moves between devices by JAX's collectives and lax.ppermute only.
A program may use at most 128 MiB of HBM per device.

v0:
```python
import math
import jax
import jax.numpy as jnp
from jax import lax
from jax.sharding import PartitionSpec as P

DIRS = 36
FREQ = 32
SUBSTEPS = 6
LAT = 128


def extended(cells, sides, width):
    for axis, dim in sides:
        count = lax.axis_size(axis)
        head = lax.slice_in_dim(cells, 0, width, axis=dim)
        tail = lax.slice_in_dim(cells, cells.shape[dim] - width, cells.shape[dim], axis=dim)
        cells = jnp.concatenate(
            [
                lax.ppermute(tail, axis, [(i, (i + 1) % count) for i in range(count)]),
                cells,
                lax.ppermute(head, axis, [((i + 1) % count, i) for i in range(count)]),
            ],
            axis=dim,
        )
    return cells


def freq_onehot(frequency):
    return (frequency[:, None] == jnp.arange(FREQ)[None, :]).astype(jnp.float32)


def flow_terms(kinds, courant):
    direction = kinds % DIRS
    frequency = kinds // DIRS
    angles = (direction.astype(jnp.float32) + 0.5) * (2.0 * math.pi / DIRS)
    speeds = jnp.dot(freq_onehot(frequency), courant, precision=lax.Precision.HIGHEST)
    latitude = (jnp.arange(LAT).astype(jnp.float32) + 0.5 - LAT / 2) * (math.pi / 2160.0)
    flow_x = speeds[:, None] * jnp.cos(angles)[:, None] / jnp.cos(latitude)[None, :]
    flow_y = speeds * jnp.sin(angles)
    return (flow_x, flow_y)


def combine(centre, from_west, from_east, rates):
    keep_rate, east_rate, west_rate, north_rate, south_rate = rates
    from_south = jnp.pad(centre[:, :-1], ((0, 0), (1, 0), (0, 0)))
    from_north = jnp.pad(centre[:, 1:], ((0, 0), (0, 1), (0, 0)))
    return (
        keep_rate * centre
        + east_rate * from_west
        + west_rate * from_east
        + north_rate * from_south
        + south_rate * from_north
    )


def propagate(wave, flow_x, flow_y, sea_mask):
    rates = (
        1.0 - jnp.abs(flow_x)[:, :, None] - jnp.abs(flow_y)[:, None, None],
        jnp.maximum(flow_x, 0.0)[:, :, None],
        jnp.maximum(-flow_x, 0.0)[:, :, None],
        jnp.maximum(flow_y, 0.0)[:, None, None],
        jnp.maximum(-flow_y, 0.0)[:, None, None],
    )
    for substep in range(SUBSTEPS):
        padded = extended(wave, (("sector", 2),), 1)
        wave = combine(wave, padded[:, :, :-2], padded[:, :, 2:], rates) * sea_mask[None]
    return wave


def local(spectrum, land_mask, wind_field, assignment, courant, growth, whitecap, weights, spread):
    member = lax.axis_index("group")
    comps_dev = spectrum.shape[0]
    lon_local = spectrum.shape[2]
    all_comps = assignment.shape[0]
    rows_dev = wind_field.shape[1]
    sea_mask = land_mask.astype(jnp.float32)
    kinds = lax.dynamic_slice_in_dim(assignment, member * comps_dev, comps_dev, 0)
    flow_x, flow_y = flow_terms(kinds, courant)
    moved = lax.all_to_all(
        propagate(spectrum, flow_x, flow_y, sea_mask),
        "group",
        split_axis=1,
        concat_axis=0,
        tiled=True,
    )
    points = rows_dev * lon_local
    energy = moved.reshape(all_comps, points)
    sea_rows = lax.dynamic_slice_in_dim(sea_mask, member * rows_dev, rows_dev, 0).reshape(points)
    winds = wind_field.reshape(2, points)
    direction = assignment % DIRS
    frequency = assignment // DIRS
    angles = (direction.astype(jnp.float32) + 0.5) * (2.0 * math.pi / DIRS)
    per_freq = jnp.stack((growth, whitecap, weights), axis=1)
    picked = jnp.dot(freq_onehot(frequency), per_freq, precision=lax.Precision.HIGHEST)
    kind_onehot = (assignment[:, None] == jnp.arange(all_comps)[None, :]).astype(jnp.float32)
    picked_rows = jnp.dot(
        kind_onehot, spread.reshape(FREQ * DIRS, DIRS), precision=lax.Precision.HIGHEST
    )
    dir_onehot = (jnp.arange(DIRS)[:, None] == direction[None, :]).astype(jnp.float32)
    same_freq = (frequency[:, None] == frequency[None, :]).astype(jnp.float32)
    coupling = jnp.dot(picked_rows, dir_onehot, precision=lax.Precision.HIGHEST) * same_freq
    loading = jnp.sum(picked[:, 2][:, None] * energy, axis=0) / all_comps
    drive = (
        jnp.cos(angles)[:, None] * winds[0][None, :] + jnp.sin(angles)[:, None] * winds[1][None, :]
    )
    exponent = (
        picked[:, 0][:, None] * jnp.maximum(drive, 0.0)
        - picked[:, 1][:, None] * (loading / (1.0 + loading))[None, :]
    )
    mixed = jnp.dot(coupling, energy, precision=lax.Precision.HIGHEST)
    renewed = (energy * jnp.exp(exponent) + 0.5 * mixed) * sea_rows[None, :]
    return lax.all_to_all(
        renewed.reshape(all_comps, rows_dev, lon_local),
        "group",
        split_axis=0,
        concat_axis=1,
        tiled=True,
    )


def solution(mesh):
    in_specs = (
        P("group", None, "sector"),
        P(None, "sector"),
        P(None, "group", "sector"),
        P(),
        P(),
        P(),
        P(),
        P(),
        P(),
    )
    out_specs = P("group", None, "sector")
    return jax.shard_map(local, mesh=mesh, in_specs=in_specs, out_specs=out_specs, check_vma=False)
```

profile of v0, /device:TPU:0, one launch (start us, length us, event | category | flops | bytes accessed | tf_op | source)
XLA Modules:
  0.0 494.8 jit_solution(8796984362894581755)
XLA Ops:
  0.0 9.6 %copy.15 = f32[144,128,128]{1,0,2:T(8,128)} copy(f32[144,128,128]{2,1,0:T(8,128)} %param.9) | data formatting | bytes 18874368 | tf_op args[0]
  15.8 14.2 %fusion.82 = (f32[144,127,128]{1,0,2:T(8,128)}, f32[144,127,128]{1,0,2:T(8,128)}) fusion(f32[144,128,128]{1,0,2:T(8,128)} %copy.15), kind=kLoop, calls=%fused_computation.122 | loop fusion | bytes 37453824 | tf_op jit(solution)/shard_map/slice | solution.py:46
  30.8 16.4 %fusion.43 = f32[144,128,128]{1,0,2:T(8,128)S(1)} fusion(f32[144,128,1]{1,0,2:T(8,128)S(1)} %collective-permute-done.1, f32[144,128,128]{1,0,2:T(8,128)} %copy.15, f32[144,128,1]{1,0,2:T(8,128)S(1)} %collective-permute-done, f32[144,127,128]{1,0,2:T(8,128)} %get-tuple-element.31, f32[144,127,128]{1,0,2:T(8,128)} %get-tuple-element.30, ...), kind=kLoop, calls=%fused_computation.57 | loop fusion | flops 28311552 | bytes 38036608 | tf_op jit(solution)/shard_map/mul | solution.py:67
  47.3 3.8 collective-permute-start.3
  51.1 8.1 %fusion.80 = (f32[144,127,128]{1,0,2:T(8,128)}, f32[144,127,128]{1,0,2:T(8,128)}) fusion(f32[144,128,128]{1,0,2:T(8,128)S(1)} %fusion.43), kind=kLoop, calls=%fused_computation.120 | loop fusion | bytes 37453824 | tf_op jit(solution)/shard_map/slice | solution.py:46
  59.2 13.2 %fusion.36 = f32[144,128,128]{1,0,2:T(8,128)} fusion(f32[144,128,1]{1,0,2:T(8,128)S(1)} %collective-permute-done.3, f32[144,128,128]{1,0,2:T(8,128)S(1)} %fusion.43, f32[144,128,1]{1,0,2:T(8,128)S(1)} %collective-permute-done.2, f32[144,127,128]{1,0,2:T(8,128)} %get-tuple-element.27, f32[144,127,128]{1,0,2:T(8,128)} %get-tuple-element.26, ...), kind=kLoop, calls=%fused_computation.48 | loop fusion | flops 28311552 | bytes 38036608 | tf_op jit(solution)/shard_map/mul | solution.py:67
  77.2 14.4 %fusion.78 = (f32[144,127,128]{1,0,2:T(8,128)}, f32[144,127,128]{1,0,2:T(8,128)}) fusion(f32[144,128,128]{1,0,2:T(8,128)} %fusion.36), kind=kLoop, calls=%fused_computation.118 | loop fusion | bytes 37453824 | tf_op jit(solution)/shard_map/slice | solution.py:46
  91.7 13.2 %fusion.29 = f32[144,128,128]{1,0,2:T(8,128)} fusion(f32[144,128,1]{1,0,2:T(8,128)S(1)} %collective-permute-done.5, f32[144,128,128]{1,0,2:T(8,128)S(1)} %bitcast.47, f32[144,128,1]{1,0,2:T(8,128)S(1)} %collective-permute-done.4, f32[144,127,128]{1,0,2:T(8,128)} %get-tuple-element.23, f32[144,127,128]{1,0,2:T(8,128)} %get-tuple-element.22, ...), kind=kLoop, calls=%fused_computation.39 | loop fusion | flops 28311552 | bytes 38036608 | tf_op jit(solution)/shard_map/mul | solution.py:67
  105.9 3.9 collective-permute-start.7
  109.9 14.4 %fusion.76 = (f32[144,127,128]{1,0,2:T(8,128)}, f32[144,127,128]{1,0,2:T(8,128)}) fusion(f32[144,128,128]{1,0,2:T(8,128)} %fusion.29), kind=kLoop, calls=%fused_computation.116 | loop fusion | bytes 37453824 | tf_op jit(solution)/shard_map/slice | solution.py:46
  124.3 13.2 %fusion.22 = f32[144,128,128]{1,0,2:T(8,128)} fusion(f32[144,128,1]{1,0,2:T(8,128)S(1)} %collective-permute-done.7, f32[144,128,128]{1,0,2:T(8,128)S(1)} %bitcast.49, f32[144,128,1]{1,0,2:T(8,128)S(1)} %collective-permute-done.6, f32[144,127,128]{1,0,2:T(8,128)} %get-tuple-element.19, f32[144,127,128]{1,0,2:T(8,128)} %get-tuple-element.18, ...), kind=kLoop, calls=%fused_computation.30 | loop fusion | flops 28311552 | bytes 38036608 | tf_op jit(solution)/shard_map/mul | solution.py:67
  142.3 14.4 %fusion.74 = (f32[144,127,128]{1,0,2:T(8,128)}, f32[144,127,128]{1,0,2:T(8,128)}) fusion(f32[144,128,128]{1,0,2:T(8,128)} %fusion.22), kind=kLoop, calls=%fused_computation.114 | loop fusion | bytes 37453824 | tf_op jit(solution)/shard_map/slice | solution.py:46
  156.8 16.4 %fusion.15 = f32[144,128,128]{1,0,2:T(8,128)S(1)} fusion(f32[144,128,1]{1,0,2:T(8,128)S(1)} %collective-permute-done.9, f32[144,128,128]{1,0,2:T(8,128)} %fusion.22, f32[144,128,1]{1,0,2:T(8,128)S(1)} %collective-permute-done.8, f32[144,127,128]{1,0,2:T(8,128)} %get-tuple-element.15, f32[144,127,128]{1,0,2:T(8,128)} %get-tuple-element.14, ...), kind=kLoop, calls=%fused_computation.21 | loop fusion | flops 28311552 | bytes 38036608 | tf_op jit(solution)/shard_map/mul | solution.py:67
  177.1 8.1 %fusion.72 = (f32[144,127,128]{1,0,2:T(8,128)}, f32[144,127,128]{1,0,2:T(8,128)}) fusion(f32[144,128,128]{1,0,2:T(8,128)S(1)} %fusion.15), kind=kLoop, calls=%fused_computation.112 | loop fusion | bytes 37453824 | tf_op jit(solution)/shard_map/slice | solution.py:46
  185.2 13.1 %fusion.8 = f32[144,128,128]{1,0,2:T(8,128)} fusion(f32[144,128,1]{1,0,2:T(8,128)S(1)} %collective-permute-done.11, f32[144,128,128]{1,0,2:T(8,128)S(1)} %fusion.15, f32[144,128,1]{1,0,2:T(8,128)S(1)} %collective-permute-done.10, f32[144,127,128]{1,0,2:T(8,128)} %get-tuple-element.11, f32[144,127,128]{1,0,2:T(8,128)} %get-tuple-element.10, ...), kind=kLoop, calls=%fused_computation.12 | loop fusion | flops 28311552 | bytes 38036608 | tf_op jit(solution)/shard_map/mul | solution.py:67
  198.3 9.6 %copy.23 = f32[144,128,128]{2,0,1:T(8,128)} copy(f32[144,128,128]{1,0,2:T(8,128)} %fusion.8) | data formatting | bytes 18874368 | tf_op jit(solution)/shard_map/mul | solution.py:67
  207.9 5.6 %all-to-all-start = ((f32[144,128,128]{2,0,1:T(8,128)}), f32[144,128,128]{2,0,1:T(8,128)}, u32[]{:S(2)}, u32[]{:S(2)}) async-start(f32[144,128,128]{2,0,1:T(8,128)} %copy.23), calls=%async_computation | async-start | bytes 18874368 | tf_op jit(solution)/shard_map/all_to_all | solution.py:80
  218.2 4.8 convolution_select_fusion
  223.0 95.8 %all-to-all-done = f32[144,128,128]{2,0,1:T(8,128)} async-done(((f32[144,128,128]{2,0,1:T(8,128)}), f32[144,128,128]{2,0,1:T(8,128)}, u32[]{:S(2)}, u32[]{:S(2)}) %all-to-all-start) | async-done | bytes 9437216 | tf_op jit(solution)/shard_map/all_to_all | solution.py:80
  318.8 6.5 %copy.24 = f32[144,8,16,128]{3,2,0,1:T(8,128)S(1)} copy(f32[144,8,16,128]{3,0,2,1:T(8,128)} %bitcast.2) | data formatting | bytes 18874368 | tf_op jit(solution)/shard_map/all_to_all | solution.py:80
  325.3 7.5 %fusion.46 = f32[16,128]{1,0:T(8,128)S(1)} fusion(f32[8,144]{1,0:T(8,128)S(1)} %mul.415, f32[144,8,16,128]{3,0,2,1:T(8,128)} %bitcast.2), kind=kLoop, calls=%fused_computation.62 | loop fusion | flops 4716544 | bytes 9449984 | tf_op jit(solution)/shard_map/reduce_sum | solution.py:103
  332.9 46.4 %fusion.3 = f32[144,8,16,128]{3,1,2,0:T(8,128)S(1)} fusion(f32[1152,1152]{1,0:T(8,128)} %convolution_select_fusion, f32[144,8,16,128]{3,2,1,0:T(8,128)S(1)} %bitcast.52, f32[2048]{0:T(1024)S(1)} %dynamic-slice_bitcast_fusion, f32[2048]{0:T(1024)S(1)} %add_divide_fusion, f32[1152]{0:T(1024)S(1)} %get-tuple-element.7, f32[2048]{0:T(1024)S(1)} %get-tuple-element.35, ...), kind=kOutput, calls=%fused_computation.6 | convolution fusion | flops 32640860160 | bytes 24233984 | tf_op jit(solution)/shard_map/dot_general | solution.py:111
  381.5 107.8 %all_to_all.33 = f32[1152,16,128]{2,1,0:T(8,128)S(1)} all-to-all(f32[1152,16,128]{2,1,0:T(8,128)S(1)} %bitcast.50), channel_id=1, replica_groups=mesh['sector'=4,'group'=8] {'group'}, dimensions={0} | all-to-all | bytes 18874368 | tf_op jit(solution)/shard_map/all_to_all | solution.py:113
  489.3 5.2 %copy.26 = f32[8,144,16,128]{3,2,0,1:T(8,128)} copy(f32[8,144,16,128]{3,2,1,0:T(8,128)S(1)} %bitcast.51) | data formatting | bytes 18874368 | tf_op jit(solution)/shard_map/all_to_all | solution.py:113
  (80 shorter events, 28.3 us)
Async XLA Ops:
  0.0 30.1 %copy-start = (f32[32]{0:T(128)S(1)}, f32[32]{0:T(128)}, u32[]{:S(2)}) copy-start(f32[32]{0:T(128)} %param.13) | copy-start | bytes 388
  10.5 20.3 %collective-permute-start = (f32[144,128,1]{1,0,2:T(8,128)S(1)}, f32[144,128,1]{1,0,2:T(8,128)S(1)}, u32[]{:S(2)}, u32[]{:S(2)}) collective-permute-start(f32[144,128,1]{1,0,2:T(8,128)S(1)} %get-tuple-element.32), channel_id=1, source_target_pairs={{0,8},{8,16},{16,24},{24,0},{1,9},{9,17},{17,25},{25,1},{2,10},{10... | collective-permute-start | bytes 221192 | tf_op jit(solution)/shard_map/ppermute | solution.py:20
  13.6 17.2 %collective-permute-start.1 = (f32[144,128,1]{1,0,2:T(8,128)S(1)}, f32[144,128,1]{1,0,2:T(8,128)S(1)}, u32[]{:S(2)}, u32[]{:S(2)}) collective-permute-start(f32[144,128,1]{1,0,2:T(8,128)S(1)} %get-tuple-element.33), channel_id=1, source_target_pairs={{8,0},{16,8},{24,16},{0,24},{9,1},{17,9},{25,17},{1,25},{10,2},{18... | collective-permute-start | bytes 221192 | tf_op jit(solution)/shard_map/ppermute | solution.py:22
  15.8 14.3 %copy-start.4 = (s32[1152]{0:T(1024)S(1)}, s32[1152]{0:T(1024)}, u32[]{:S(2)}) copy-start(s32[1152]{0:T(1024)} %param.12) | copy-start | bytes 13828
  15.8 14.9 %copy-start.3 = (s32[128,128]{1,0:T(8,128)S(1)}, s32[128,128]{1,0:T(8,128)}, u32[]{:S(2)}) copy-start(s32[128,128]{1,0:T(8,128)} %param.10) | copy-start | bytes 196612
  47.2 12.0 %collective-permute-start.2 = (f32[144,128,1]{1,0,2:T(8,128)S(1)}, f32[144,128,1]{1,0,2:T(8,128)S(1)}, u32[]{:S(2)}, u32[]{:S(2)}) collective-permute-start(f32[144,128,1]{1,0,2:T(8,128)S(1)} %get-tuple-element.28), channel_id=1, source_target_pairs={{0,8},{8,16},{16,24},{24,0},{1,9},{9,17},{17,25},{25,1},{2,10},{10... | collective-permute-start | bytes 221192 | tf_op jit(solution)/shard_map/ppermute | solution.py:20
  47.3 11.9 %collective-permute-start.3 = (f32[144,128,1]{1,0,2:T(8,128)S(1)}, f32[144,128,1]{1,0,2:T(8,128)S(1)}, u32[]{:S(2)}, u32[]{:S(2)}) collective-permute-start(f32[144,128,1]{1,0,2:T(8,128)S(1)} %get-tuple-element.29), channel_id=1, source_target_pairs={{8,0},{16,8},{24,16},{0,24},{9,1},{17,9},{25,17},{1,25},{10,2},{18... | collective-permute-start | bytes 221192 | tf_op jit(solution)/shard_map/ppermute | solution.py:22
  73.3 18.3 %collective-permute-start.4 = (f32[144,128,1]{1,0,2:T(8,128)S(1)}, f32[144,128,1]{1,0,2:T(8,128)S(1)}, u32[]{:S(2)}, u32[]{:S(2)}) collective-permute-start(f32[144,128,1]{1,0,2:T(8,128)S(1)} %get-tuple-element.24), channel_id=1, source_target_pairs={{0,8},{8,16},{16,24},{24,0},{1,9},{9,17},{17,25},{25,1},{2,10},{10... | collective-permute-start | bytes 221192 | tf_op jit(solution)/shard_map/ppermute | solution.py:20
  73.4 18.2 %slice-start = ((s8[9437184]{0:T(1024)(128)(4,1)}), s8[4194304]{0:T(1024)(128)(4,1)S(1)}, s32[]{:S(2)}) async-start(s8[9437184]{0:T(1024)(128)(4,1)} %bitcast.46), calls=%async_computation.2 | async-start | bytes 8388608
  73.4 18.2 %slice-start.1 = ((s8[9437184]{0:T(1024)(128)(4,1)}), s8[4194304]{0:T(1024)(128)(4,1)S(1)}, s32[]{:S(2)}) async-start(s8[9437184]{0:T(1024)(128)(4,1)} %bitcast.46), calls=%async_computation.3 | async-start | bytes 8388608
  73.4 18.2 %slice-start.2 = ((s8[9437184]{0:T(1024)(128)(4,1)}), s8[1048576]{0:T(1024)(128)(4,1)S(1)}, s32[]{:S(2)}) async-start(s8[9437184]{0:T(1024)(128)(4,1)} %bitcast.46), calls=%async_computation.4 | async-start | bytes 2097152
  73.4 18.2 %collective-permute-start.5 = (f32[144,128,1]{1,0,2:T(8,128)S(1)}, f32[144,128,1]{1,0,2:T(8,128)S(1)}, u32[]{:S(2)}, u32[]{:S(2)}) collective-permute-start(f32[144,128,1]{1,0,2:T(8,128)S(1)} %get-tuple-element.25), channel_id=1, source_target_pairs={{8,0},{16,8},{24,16},{0,24},{9,1},{17,9},{25,17},{1,25},{10,2},{18... | collective-permute-start | bytes 221192 | tf_op jit(solution)/shard_map/ppermute | solution.py:22
  105.8 18.5 %collective-permute-start.6 = (f32[144,128,1]{1,0,2:T(8,128)S(1)}, f32[144,128,1]{1,0,2:T(8,128)S(1)}, u32[]{:S(2)}, u32[]{:S(2)}) collective-permute-start(f32[144,128,1]{1,0,2:T(8,128)S(1)} %get-tuple-element.20), channel_id=1, source_target_pairs={{0,8},{8,16},{16,24},{24,0},{1,9},{9,17},{17,25},{25,1},{2,10},{10... | collective-permute-start | bytes 221192 | tf_op jit(solution)/shard_map/ppermute | solution.py:20
  105.9 18.4 %slice-start.3 = ((s8[9437184]{0:T(1024)(128)(4,1)}), s8[4194304]{0:T(1024)(128)(4,1)S(1)}, s32[]{:S(2)}) async-start(s8[9437184]{0:T(1024)(128)(4,1)} %bitcast.48), calls=%async_computation.5 | async-start | bytes 8388608
  105.9 18.4 %slice-start.4 = ((s8[9437184]{0:T(1024)(128)(4,1)}), s8[4194304]{0:T(1024)(128)(4,1)S(1)}, s32[]{:S(2)}) async-start(s8[9437184]{0:T(1024)(128)(4,1)} %bitcast.48), calls=%async_computation.6 | async-start | bytes 8388608
  105.9 18.4 %slice-start.5 = ((s8[9437184]{0:T(1024)(128)(4,1)}), s8[1048576]{0:T(1024)(128)(4,1)S(1)}, s32[]{:S(2)}) async-start(s8[9437184]{0:T(1024)(128)(4,1)} %bitcast.48), calls=%async_computation.7 | async-start | bytes 2097152
  105.9 18.4 %collective-permute-start.7 = (f32[144,128,1]{1,0,2:T(8,128)S(1)}, f32[144,128,1]{1,0,2:T(8,128)S(1)}, u32[]{:S(2)}, u32[]{:S(2)}) collective-permute-start(f32[144,128,1]{1,0,2:T(8,128)S(1)} %get-tuple-element.21), channel_id=1, source_target_pairs={{8,0},{16,8},{24,16},{0,24},{9,1},{17,9},{25,17},{1,25},{10,2},{18... | collective-permute-start | bytes 221192 | tf_op jit(solution)/shard_map/ppermute | solution.py:22
  138.5 18.3 %collective-permute-start.8 = (f32[144,128,1]{1,0,2:T(8,128)S(1)}, f32[144,128,1]{1,0,2:T(8,128)S(1)}, u32[]{:S(2)}, u32[]{:S(2)}) collective-permute-start(f32[144,128,1]{1,0,2:T(8,128)S(1)} %get-tuple-element.16), channel_id=1, source_target_pairs={{0,8},{8,16},{16,24},{24,0},{1,9},{9,17},{17,25},{25,1},{2,10},{10... | collective-permute-start | bytes 221192 | tf_op jit(solution)/shard_map/ppermute | solution.py:20
  138.5 18.2 %collective-permute-start.9 = (f32[144,128,1]{1,0,2:T(8,128)S(1)}, f32[144,128,1]{1,0,2:T(8,128)S(1)}, u32[]{:S(2)}, u32[]{:S(2)}) collective-permute-start(f32[144,128,1]{1,0,2:T(8,128)S(1)} %get-tuple-element.17), channel_id=1, source_target_pairs={{8,0},{16,8},{24,16},{0,24},{9,1},{17,9},{25,17},{1,25},{10,2},{18... | collective-permute-start | bytes 221192 | tf_op jit(solution)/shard_map/ppermute | solution.py:22
  173.2 12.0 %collective-permute-start.10 = (f32[144,128,1]{1,0,2:T(8,128)S(1)}, f32[144,128,1]{1,0,2:T(8,128)S(1)}, u32[]{:S(2)}, u32[]{:S(2)}) collective-permute-start(f32[144,128,1]{1,0,2:T(8,128)S(1)} %get-tuple-element.12), channel_id=1, source_target_pairs={{0,8},{8,16},{16,24},{24,0},{1,9},{9,17},{17,25},{25,1},{2,10},{10... | collective-permute-start | bytes 221192 | tf_op jit(solution)/shard_map/ppermute | solution.py:20
  173.2 11.9 %collective-permute-start.11 = (f32[144,128,1]{1,0,2:T(8,128)S(1)}, f32[144,128,1]{1,0,2:T(8,128)S(1)}, u32[]{:S(2)}, u32[]{:S(2)}) collective-permute-start(f32[144,128,1]{1,0,2:T(8,128)S(1)} %get-tuple-element.13), channel_id=1, source_target_pairs={{8,0},{16,8},{24,16},{0,24},{9,1},{17,9},{25,17},{1,25},{10,2},{18... | collective-permute-start | bytes 221192 | tf_op jit(solution)/shard_map/ppermute | solution.py:22
  207.9 6.3 %copy-start.2 = (f32[32,36,36]{2,0,1:T(8,128)S(1)}, f32[32,36,36]{2,0,1:T(8,128)}, u32[]{:S(2)}) copy-start(f32[32,36,36]{2,0,1:T(8,128)} %param.17) | copy-start | bytes 497668
  207.9 7.5 %copy-start.5 = (f32[2,16,128]{2,1,0:T(8,128)S(1)}, f32[2,16,128]{2,1,0:T(8,128)}, u32[]{:S(2)}) copy-start(f32[2,16,128]{2,1,0:T(8,128)} %param.11) | copy-start | bytes 49156
  207.9 110.9 %all-to-all-start = ((f32[144,128,128]{2,0,1:T(8,128)}), f32[144,128,128]{2,0,1:T(8,128)}, u32[]{:S(2)}, u32[]{:S(2)}) async-start(f32[144,128,128]{2,0,1:T(8,128)} %copy.23), calls=%async_computation | async-start | bytes 18874368 | tf_op jit(solution)/shard_map/all_to_all | solution.py:80
  (4 other events, 22.3 us)
where the time goes:
time: 503 us; the launch traced here: 495 us
  local copies, waits for them, and re-layouts  112 us (22%)
  blocking collectives  108 us (21%)
  waiting for transfers between devices  95.8 us (19%)
  other arithmetic  93.6 us (19%)
  matrix products  54.6 us (11%)
  starting transfers between devices  30.3 us (6%)
    all_to_all x1, blocking collectives, local(): lax.all_to_all(renewed.reshape(all_comps, rows_dev, lon_local), 'group',...  108 us
    all_to_all x1, waiting for transfers between devices, local(): lax.all_to_all(propagate(spectrum, flow_x, flow_y, sea_mask), 'group', sp...  95.8 us
    mul x6, other arithmetic, propagate(): combine(wave, padded[:, :, :-2], padded[:, :, 2:], rates) * sea_mask[None]  85.5 us
    slice x6, local copies, waits for them, and re-layouts, combine(): from_south = jnp.pad(centre[:, :-1], ((0, 0), (1, 0), (0, 0)))  73.7 us
    dot_general x1, matrix products, local(): mixed = jnp.dot(coupling, energy, precision=lax.Precision.HIGHEST)  46.4 us
    ppermute x6, starting transfers between devices, extended(): lax.ppermute(head, axis, [((i + 1) % count, i) for i in range(count)])  21.2 us
    unnamed x33, local copies, waits for them, and re-layouts  12.7 us
  transfers between devices with their start and end apart: 13, of which 1 were waited for; matrix products, arithmetic and copies ran while one was open for 17% of the time, Pallas kernels for 0%

commit v1 on v0

--- a/solution.py
+++ b/solution.py
@@ -110,12 +110,18 @@
     )
     mixed = jnp.dot(coupling, energy, precision=lax.Precision.HIGHEST)
     renewed = (energy * jnp.exp(exponent) + 0.5 * mixed) * sea_rows[None, :]
-    return lax.all_to_all(
-        renewed.reshape(all_comps, rows_dev, lon_local),
-        "group",
-        split_axis=0,
-        concat_axis=1,
-        tiled=True,
+    return jnp.concatenate(
+        lax.all_to_all(
+            jnp.stack(
+                jnp.split(
+                    renewed.reshape(all_comps, rows_dev, lon_local), lax.axis_size("group"), axis=0
+                )
+            ),
+            "group",
+            0,
+            0,
+        ),
+        axis=1,
     )
 
 

time: 503 us -> 504 us (level)
    all_to_all x1 -> x0, local copies, waits for them, and re-layouts: 5.2 us -> none  [local(): lax.all_to_all(renewed.reshape(all_comps, rows_dev, lon_local), 'group',...]
    reshape x0 -> x1, local copies, waits for them, and re-layouts: none -> 5.2 us  [local(): jnp.concatenate(lax.all_to_all(jnp.stack(jnp.split(renewed.reshape(all_co...]
    unnamed x33 -> x48, local copies, waits for them, and re-layouts: 12.7 us -> 14 us
where the time goes in v1:
time: 504 us; the launch traced here: 496 us
  local copies, waits for them, and re-layouts  113 us (22%)
  blocking collectives  108 us (21%)
  waiting for transfers between devices  95.8 us (19%)
  other arithmetic  93.3 us (19%)
  matrix products  54.7 us (11%)
  starting transfers between devices  30.3 us (6%)
    all_to_all x1, blocking collectives, local(): lax.all_to_all(jnp.stack(jnp.split(renewed.reshape(all_comps, rows_dev, l...  108 us
    all_to_all x1, waiting for transfers between devices, local(): lax.all_to_all(propagate(spectrum, flow_x, flow_y, sea_mask), 'group', sp...  95.8 us
    mul x6, other arithmetic, propagate(): combine(wave, padded[:, :, :-2], padded[:, :, 2:], rates) * sea_mask[None]  85.2 us
    slice x6, local copies, waits for them, and re-layouts, combine(): from_south = jnp.pad(centre[:, :-1], ((0, 0), (1, 0), (0, 0)))  73.7 us
    dot_general x1, matrix products, local(): mixed = jnp.dot(coupling, energy, precision=lax.Precision.HIGHEST)  46.4 us
    ppermute x6, starting transfers between devices, extended(): lax.ppermute(head, axis, [((i + 1) % count, i) for i in range(count)])  21.2 us
    unnamed x48, local copies, waits for them, and re-layouts  14 us
  transfers between devices with their start and end apart: 13, of which 1 were waited for; matrix products, arithmetic and copies ran while one was open for 17% of the time, Pallas kernels for 0%

profile of v1, /device:TPU:0, one launch (start us, length us, event | category | flops | bytes accessed | tf_op | source)
XLA Modules:
  0.0 496.1 jit_solution(61934045604755149)
XLA Ops:
  0.0 9.6 %copy.15 = f32[144,128,128]{1,0,2:T(8,128)} copy(f32[144,128,128]{2,1,0:T(8,128)} %param.9) | data formatting | bytes 18874368 | tf_op args[0]
  15.8 14.2 %fusion.81 = (f32[144,127,128]{1,0,2:T(8,128)}, f32[144,127,128]{1,0,2:T(8,128)}) fusion(f32[144,128,128]{1,0,2:T(8,128)} %copy.15), kind=kLoop, calls=%fused_computation.137 | loop fusion | bytes 37453824 | tf_op jit(solution)/shard_map/slice | solution.py:46
  30.8 16.4 %fusion.42 = f32[144,128,128]{1,0,2:T(8,128)S(1)} fusion(f32[144,128,1]{1,0,2:T(8,128)S(1)} %collective-permute-done.1, f32[144,128,128]{1,0,2:T(8,128)} %copy.15, f32[144,128,1]{1,0,2:T(8,128)S(1)} %collective-permute-done, f32[144,127,128]{1,0,2:T(8,128)} %get-tuple-element.39, f32[144,127,128]{1,0,2:T(8,128)} %get-tuple-element.38, ...), kind=kLoop, calls=%fused_computation.56 | loop fusion | flops 28311552 | bytes 38036608 | tf_op jit(solution)/shard_map/mul | solution.py:67
  51.1 8.1 %fusion.79 = (f32[144,127,128]{1,0,2:T(8,128)}, f32[144,127,128]{1,0,2:T(8,128)}) fusion(f32[144,128,128]{1,0,2:T(8,128)S(1)} %fusion.42), kind=kLoop, calls=%fused_computation.135 | loop fusion | bytes 37453824 | tf_op jit(solution)/shard_map/slice | solution.py:46
  59.2 13.1 %fusion.35 = f32[144,128,128]{1,0,2:T(8,128)} fusion(f32[144,128,1]{1,0,2:T(8,128)S(1)} %collective-permute-done.3, f32[144,128,128]{1,0,2:T(8,128)S(1)} %fusion.42, f32[144,128,1]{1,0,2:T(8,128)S(1)} %collective-permute-done.2, f32[144,127,128]{1,0,2:T(8,128)} %get-tuple-element.35, f32[144,127,128]{1,0,2:T(8,128)} %get-tuple-element.34, ...), kind=kLoop, calls=%fused_computation.47 | loop fusion | flops 28311552 | bytes 38036608 | tf_op jit(solution)/shard_map/mul | solution.py:67
  77.1 14.4 %fusion.77 = (f32[144,127,128]{1,0,2:T(8,128)}, f32[144,127,128]{1,0,2:T(8,128)}) fusion(f32[144,128,128]{1,0,2:T(8,128)} %fusion.35), kind=kLoop, calls=%fused_computation.133 | loop fusion | bytes 37453824 | tf_op jit(solution)/shard_map/slice | solution.py:46
  91.6 13.1 %fusion.28 = f32[144,128,128]{1,0,2:T(8,128)} fusion(f32[144,128,1]{1,0,2:T(8,128)S(1)} %collective-permute-done.5, f32[144,128,128]{1,0,2:T(8,128)S(1)} %bitcast.88, f32[144,128,1]{1,0,2:T(8,128)S(1)} %collective-permute-done.4, f32[144,127,128]{1,0,2:T(8,128)} %get-tuple-element.31, f32[144,127,128]{1,0,2:T(8,128)} %get-tuple-element.30, ...), kind=kLoop, calls=%fused_computation.38 | loop fusion | flops 28311552 | bytes 38036608 | tf_op jit(solution)/shard_map/mul | solution.py:67
  105.8 3.9 collective-permute-start.7
  109.7 14.4 %fusion.75 = (f32[144,127,128]{1,0,2:T(8,128)}, f32[144,127,128]{1,0,2:T(8,128)}) fusion(f32[144,128,128]{1,0,2:T(8,128)} %fusion.28), kind=kLoop, calls=%fused_computation.131 | loop fusion | bytes 37453824 | tf_op jit(solution)/shard_map/slice | solution.py:46
  124.2 13.1 %fusion.21 = f32[144,128,128]{1,0,2:T(8,128)} fusion(f32[144,128,1]{1,0,2:T(8,128)S(1)} %collective-permute-done.7, f32[144,128,128]{1,0,2:T(8,128)S(1)} %bitcast.90, f32[144,128,1]{1,0,2:T(8,128)S(1)} %collective-permute-done.6, f32[144,127,128]{1,0,2:T(8,128)} %get-tuple-element.27, f32[144,127,128]{1,0,2:T(8,128)} %get-tuple-element.26, ...), kind=kLoop, calls=%fused_computation.29 | loop fusion | flops 28311552 | bytes 38036608 | tf_op jit(solution)/shard_map/mul | solution.py:67
  142.1 14.4 %fusion.73 = (f32[144,127,128]{1,0,2:T(8,128)}, f32[144,127,128]{1,0,2:T(8,128)}) fusion(f32[144,128,128]{1,0,2:T(8,128)} %fusion.21), kind=kLoop, calls=%fused_computation.129 | loop fusion | bytes 37453824 | tf_op jit(solution)/shard_map/slice | solution.py:46
  156.5 16.4 %fusion.14 = f32[144,128,128]{1,0,2:T(8,128)S(1)} fusion(f32[144,128,1]{1,0,2:T(8,128)S(1)} %collective-permute-done.9, f32[144,128,128]{1,0,2:T(8,128)} %fusion.21, f32[144,128,1]{1,0,2:T(8,128)S(1)} %collective-permute-done.8, f32[144,127,128]{1,0,2:T(8,128)} %get-tuple-element.23, f32[144,127,128]{1,0,2:T(8,128)} %get-tuple-element.22, ...), kind=kLoop, calls=%fused_computation.20 | loop fusion | flops 28311552 | bytes 38036608 | tf_op jit(solution)/shard_map/mul | solution.py:67
  173.0 3.8 collective-permute-start.11
  176.8 8.1 %fusion.71 = (f32[144,127,128]{1,0,2:T(8,128)}, f32[144,127,128]{1,0,2:T(8,128)}) fusion(f32[144,128,128]{1,0,2:T(8,128)S(1)} %fusion.14), kind=kLoop, calls=%fused_computation.127 | loop fusion | bytes 37453824 | tf_op jit(solution)/shard_map/slice | solution.py:46
  184.9 13.1 %fusion.7 = f32[144,128,128]{1,0,2:T(8,128)} fusion(f32[144,128,1]{1,0,2:T(8,128)S(1)} %collective-permute-done.11, f32[144,128,128]{1,0,2:T(8,128)S(1)} %fusion.14, f32[144,128,1]{1,0,2:T(8,128)S(1)} %collective-permute-done.10, f32[144,127,128]{1,0,2:T(8,128)} %get-tuple-element.19, f32[144,127,128]{1,0,2:T(8,128)} %get-tuple-element.18, ...), kind=kLoop, calls=%fused_computation.11 | loop fusion | flops 28311552 | bytes 38036608 | tf_op jit(solution)/shard_map/mul | solution.py:67
  198.0 9.6 %copy.23 = f32[144,128,128]{2,0,1:T(8,128)} copy(f32[144,128,128]{1,0,2:T(8,128)} %fusion.7) | data formatting | bytes 18874368 | tf_op jit(solution)/shard_map/mul | solution.py:67
  207.7 5.6 %all-to-all-start = ((f32[144,128,128]{2,0,1:T(8,128)}), f32[144,128,128]{2,0,1:T(8,128)}, u32[]{:S(2)}, u32[]{:S(2)}) async-start(f32[144,128,128]{2,0,1:T(8,128)} %copy.23), calls=%async_computation | async-start | bytes 18874368 | tf_op jit(solution)/shard_map/all_to_all | solution.py:80
  217.9 4.8 convolution_select_fusion
  222.8 95.8 %all-to-all-done = f32[144,128,128]{2,0,1:T(8,128)} async-done(((f32[144,128,128]{2,0,1:T(8,128)}), f32[144,128,128]{2,0,1:T(8,128)}, u32[]{:S(2)}, u32[]{:S(2)}) %all-to-all-start) | async-done | bytes 9437216 | tf_op jit(solution)/shard_map/all_to_all | solution.py:80
  318.6 6.5 %copy.24 = f32[144,8,16,128]{3,2,0,1:T(8,128)S(1)} copy(f32[144,8,16,128]{3,0,2,1:T(8,128)} %bitcast.2) | data formatting | bytes 18874368 | tf_op jit(solution)/shard_map/all_to_all | solution.py:80
  325.1 7.5 %fusion.45 = f32[16,128]{1,0:T(8,128)S(1)} fusion(f32[8,144]{1,0:T(8,128)S(1)} %mul.415, f32[144,8,16,128]{3,0,2,1:T(8,128)} %bitcast.2), kind=kLoop, calls=%fused_computation.61 | loop fusion | flops 4716544 | bytes 9449984 | tf_op jit(solution)/shard_map/reduce_sum | solution.py:103
  332.6 46.4 %fusion.2 = f32[1152,2048]{1,0:T(8,128)S(1)} fusion(f32[1152,1152]{1,0:T(8,128)} %convolution_select_fusion, f32[144,8,16,128]{3,2,1,0:T(8,128)S(1)} %bitcast.92, f32[2048]{0:T(1024)S(1)} %dynamic-slice_bitcast_fusion, f32[2048]{0:T(1024)S(1)} %add_divide_fusion, f32[1152]{0:T(1024)S(1)} %get-tuple-element.7, f32[2048]{0:T(1024)S(1)} %get-tuple-element.43, ...), kind=kOutput, calls=%fused_computation.5 | convolution fusion | flops 32640860160 | bytes 24233984 | tf_op jit(solution)/shard_map/dot_general | solution.py:111
  382.8 107.8 %all_to_all.20 = f32[8,144,16,128]{3,2,1,0:T(8,128)S(1)} all-to-all(f32[8,144,16,128]{3,2,1,0:T(8,128)S(1)} %bitcast_dynamic-update-slice_fusion), channel_id=1, replica_groups=mesh['sector'=4,'group'=8] {'group'}, dimensions={0} | all-to-all | bytes 18874368 | tf_op jit(solution)/shard_map/all_to_all | solution.py:114
  490.7 5.2 %copy.26 = f32[144,8,16,128]{3,2,1,0:T(8,128)} copy(f32[144,8,16,128]{3,2,0,1:T(8,128)S(1)} %bitcast.91) | data formatting | bytes 18874368 | tf_op jit(solution)/shard_map/reshape | solution.py:113
  (96 shorter events, 29.7 us)
Async XLA Ops:
  0.0 30.1 %copy-start = (f32[32]{0:T(128)S(1)}, f32[32]{0:T(128)}, u32[]{:S(2)}) copy-start(f32[32]{0:T(128)} %param.13) | copy-start | bytes 388
  10.5 20.3 %collective-permute-start = (f32[144,128,1]{1,0,2:T(8,128)S(1)}, f32[144,128,1]{1,0,2:T(8,128)S(1)}, u32[]{:S(2)}, u32[]{:S(2)}) collective-permute-start(f32[144,128,1]{1,0,2:T(8,128)S(1)} %get-tuple-element.40), channel_id=1, source_target_pairs={{0,8},{8,16},{16,24},{24,0},{1,9},{9,17},{17,25},{25,1},{2,10},{10... | collective-permute-start | bytes 221192 | tf_op jit(solution)/shard_map/ppermute | solution.py:20
  13.6 17.2 %collective-permute-start.1 = (f32[144,128,1]{1,0,2:T(8,128)S(1)}, f32[144,128,1]{1,0,2:T(8,128)S(1)}, u32[]{:S(2)}, u32[]{:S(2)}) collective-permute-start(f32[144,128,1]{1,0,2:T(8,128)S(1)} %get-tuple-element.41), channel_id=1, source_target_pairs={{8,0},{16,8},{24,16},{0,24},{9,1},{17,9},{25,17},{1,25},{10,2},{18... | collective-permute-start | bytes 221192 | tf_op jit(solution)/shard_map/ppermute | solution.py:22
  15.8 14.3 %copy-start.4 = (s32[1152]{0:T(1024)S(1)}, s32[1152]{0:T(1024)}, u32[]{:S(2)}) copy-start(s32[1152]{0:T(1024)} %param.12) | copy-start | bytes 13828
  15.8 14.9 %copy-start.3 = (s32[128,128]{1,0:T(8,128)S(1)}, s32[128,128]{1,0:T(8,128)}, u32[]{:S(2)}) copy-start(s32[128,128]{1,0:T(8,128)} %param.10) | copy-start | bytes 196612
  47.2 12.0 %collective-permute-start.2 = (f32[144,128,1]{1,0,2:T(8,128)S(1)}, f32[144,128,1]{1,0,2:T(8,128)S(1)}, u32[]{:S(2)}, u32[]{:S(2)}) collective-permute-start(f32[144,128,1]{1,0,2:T(8,128)S(1)} %get-tuple-element.36), channel_id=1, source_target_pairs={{0,8},{8,16},{16,24},{24,0},{1,9},{9,17},{17,25},{25,1},{2,10},{10... | collective-permute-start | bytes 221192 | tf_op jit(solution)/shard_map/ppermute | solution.py:20
  47.3 11.9 %collective-permute-start.3 = (f32[144,128,1]{1,0,2:T(8,128)S(1)}, f32[144,128,1]{1,0,2:T(8,128)S(1)}, u32[]{:S(2)}, u32[]{:S(2)}) collective-permute-start(f32[144,128,1]{1,0,2:T(8,128)S(1)} %get-tuple-element.37), channel_id=1, source_target_pairs={{8,0},{16,8},{24,16},{0,24},{9,1},{17,9},{25,17},{1,25},{10,2},{18... | collective-permute-start | bytes 221192 | tf_op jit(solution)/shard_map/ppermute | solution.py:22
  73.2 18.3 %collective-permute-start.4 = (f32[144,128,1]{1,0,2:T(8,128)S(1)}, f32[144,128,1]{1,0,2:T(8,128)S(1)}, u32[]{:S(2)}, u32[]{:S(2)}) collective-permute-start(f32[144,128,1]{1,0,2:T(8,128)S(1)} %get-tuple-element.32), channel_id=1, source_target_pairs={{0,8},{8,16},{16,24},{24,0},{1,9},{9,17},{17,25},{25,1},{2,10},{10... | collective-permute-start | bytes 221192 | tf_op jit(solution)/shard_map/ppermute | solution.py:20
  73.3 18.2 %slice-start = ((s8[9437184]{0:T(1024)(128)(4,1)}), s8[4194304]{0:T(1024)(128)(4,1)S(1)}, s32[]{:S(2)}) async-start(s8[9437184]{0:T(1024)(128)(4,1)} %bitcast.87), calls=%async_computation.2 | async-start | bytes 8388608
  73.3 18.2 %slice-start.1 = ((s8[9437184]{0:T(1024)(128)(4,1)}), s8[4194304]{0:T(1024)(128)(4,1)S(1)}, s32[]{:S(2)}) async-start(s8[9437184]{0:T(1024)(128)(4,1)} %bitcast.87), calls=%async_computation.3 | async-start | bytes 8388608
  73.3 18.2 %slice-start.2 = ((s8[9437184]{0:T(1024)(128)(4,1)}), s8[1048576]{0:T(1024)(128)(4,1)S(1)}, s32[]{:S(2)}) async-start(s8[9437184]{0:T(1024)(128)(4,1)} %bitcast.87), calls=%async_computation.4 | async-start | bytes 2097152
  73.3 18.2 %collective-permute-start.5 = (f32[144,128,1]{1,0,2:T(8,128)S(1)}, f32[144,128,1]{1,0,2:T(8,128)S(1)}, u32[]{:S(2)}, u32[]{:S(2)}) collective-permute-start(f32[144,128,1]{1,0,2:T(8,128)S(1)} %get-tuple-element.33), channel_id=1, source_target_pairs={{8,0},{16,8},{24,16},{0,24},{9,1},{17,9},{25,17},{1,25},{10,2},{18... | collective-permute-start | bytes 221192 | tf_op jit(solution)/shard_map/ppermute | solution.py:22
  105.7 18.5 %collective-permute-start.6 = (f32[144,128,1]{1,0,2:T(8,128)S(1)}, f32[144,128,1]{1,0,2:T(8,128)S(1)}, u32[]{:S(2)}, u32[]{:S(2)}) collective-permute-start(f32[144,128,1]{1,0,2:T(8,128)S(1)} %get-tuple-element.28), channel_id=1, source_target_pairs={{0,8},{8,16},{16,24},{24,0},{1,9},{9,17},{17,25},{25,1},{2,10},{10... | collective-permute-start | bytes 221192 | tf_op jit(solution)/shard_map/ppermute | solution.py:20
  105.7 18.4 %slice-start.3 = ((s8[9437184]{0:T(1024)(128)(4,1)}), s8[4194304]{0:T(1024)(128)(4,1)S(1)}, s32[]{:S(2)}) async-start(s8[9437184]{0:T(1024)(128)(4,1)} %bitcast.89), calls=%async_computation.5 | async-start | bytes 8388608
  105.7 18.4 %slice-start.4 = ((s8[9437184]{0:T(1024)(128)(4,1)}), s8[4194304]{0:T(1024)(128)(4,1)S(1)}, s32[]{:S(2)}) async-start(s8[9437184]{0:T(1024)(128)(4,1)} %bitcast.89), calls=%async_computation.6 | async-start | bytes 8388608
  105.7 18.4 %slice-start.5 = ((s8[9437184]{0:T(1024)(128)(4,1)}), s8[1048576]{0:T(1024)(128)(4,1)S(1)}, s32[]{:S(2)}) async-start(s8[9437184]{0:T(1024)(128)(4,1)} %bitcast.89), calls=%async_computation.7 | async-start | bytes 2097152
  105.8 18.4 %collective-permute-start.7 = (f32[144,128,1]{1,0,2:T(8,128)S(1)}, f32[144,128,1]{1,0,2:T(8,128)S(1)}, u32[]{:S(2)}, u32[]{:S(2)}) collective-permute-start(f32[144,128,1]{1,0,2:T(8,128)S(1)} %get-tuple-element.29), channel_id=1, source_target_pairs={{8,0},{16,8},{24,16},{0,24},{9,1},{17,9},{25,17},{1,25},{10,2},{18... | collective-permute-start | bytes 221192 | tf_op jit(solution)/shard_map/ppermute | solution.py:22
  138.2 18.3 %collective-permute-start.8 = (f32[144,128,1]{1,0,2:T(8,128)S(1)}, f32[144,128,1]{1,0,2:T(8,128)S(1)}, u32[]{:S(2)}, u32[]{:S(2)}) collective-permute-start(f32[144,128,1]{1,0,2:T(8,128)S(1)} %get-tuple-element.24), channel_id=1, source_target_pairs={{0,8},{8,16},{16,24},{24,0},{1,9},{9,17},{17,25},{25,1},{2,10},{10... | collective-permute-start | bytes 221192 | tf_op jit(solution)/shard_map/ppermute | solution.py:20
  138.3 18.2 %collective-permute-start.9 = (f32[144,128,1]{1,0,2:T(8,128)S(1)}, f32[144,128,1]{1,0,2:T(8,128)S(1)}, u32[]{:S(2)}, u32[]{:S(2)}) collective-permute-start(f32[144,128,1]{1,0,2:T(8,128)S(1)} %get-tuple-element.25), channel_id=1, source_target_pairs={{8,0},{16,8},{24,16},{0,24},{9,1},{17,9},{25,17},{1,25},{10,2},{18... | collective-permute-start | bytes 221192 | tf_op jit(solution)/shard_map/ppermute | solution.py:22
  172.9 12.0 %collective-permute-start.10 = (f32[144,128,1]{1,0,2:T(8,128)S(1)}, f32[144,128,1]{1,0,2:T(8,128)S(1)}, u32[]{:S(2)}, u32[]{:S(2)}) collective-permute-start(f32[144,128,1]{1,0,2:T(8,128)S(1)} %get-tuple-element.20), channel_id=1, source_target_pairs={{0,8},{8,16},{16,24},{24,0},{1,9},{9,17},{17,25},{25,1},{2,10},{10... | collective-permute-start | bytes 221192 | tf_op jit(solution)/shard_map/ppermute | solution.py:20
  173.0 11.9 %collective-permute-start.11 = (f32[144,128,1]{1,0,2:T(8,128)S(1)}, f32[144,128,1]{1,0,2:T(8,128)S(1)}, u32[]{:S(2)}, u32[]{:S(2)}) collective-permute-start(f32[144,128,1]{1,0,2:T(8,128)S(1)} %get-tuple-element.21), channel_id=1, source_target_pairs={{8,0},{16,8},{24,16},{0,24},{9,1},{17,9},{25,17},{1,25},{10,2},{18... | collective-permute-start | bytes 221192 | tf_op jit(solution)/shard_map/ppermute | solution.py:22
  207.7 6.3 %copy-start.2 = (f32[32,36,36]{2,0,1:T(8,128)S(1)}, f32[32,36,36]{2,0,1:T(8,128)}, u32[]{:S(2)}) copy-start(f32[32,36,36]{2,0,1:T(8,128)} %param.17) | copy-start | bytes 497668
  207.7 7.5 %copy-start.5 = (f32[2,16,128]{2,1,0:T(8,128)S(1)}, f32[2,16,128]{2,1,0:T(8,128)}, u32[]{:S(2)}) copy-start(f32[2,16,128]{2,1,0:T(8,128)} %param.11) | copy-start | bytes 49156
  207.7 110.9 %all-to-all-start = ((f32[144,128,128]{2,0,1:T(8,128)}), f32[144,128,128]{2,0,1:T(8,128)}, u32[]{:S(2)}, u32[]{:S(2)}) async-start(f32[144,128,128]{2,0,1:T(8,128)} %copy.23), calls=%async_computation | async-start | bytes 18874368 | tf_op jit(solution)/shard_map/all_to_all | solution.py:80
  (4 other events, 22.2 us)
